TPU v7x, 32 devices: a whole 2x2x4 slice. The times are simulated.
32 devices in a mesh: row: 8 (over z, x), col: 4 (over y, core).
Axes of the slice: x: 2, y: 2, z: 4, core: 2. Of those that a mesh axis runs over, the one named last changes fastest.
Arguments:
- blocks: bfloat16 [8, 4, 256, 128, 128], P('row', 'col'), may hold values from -0.25 to 0.25
- block_rows: int32 [8, 4, 256], P('row', 'col'), may hold values from 0 to 255
- block_cols: int32 [8, 4, 256], P('row', 'col'), may hold values from 0 to 255
- counts: int32 [8, 4], P('row', 'col'), may hold values from 85 to 256, as said below
- data: float32 [262144], P('row'), may hold values from -16 to 16
Outputs:
- solution: float32 [131072], P('col')
- search: float32 [131072], P('col')
- data_basis: float32 [262144], P('row')
Inputs may be any that keep to these rules, and one draw needn't show every extreme that they name: `counts`: every tile has between 85 and 256 live slots; some tile has exactly 256.
All inputs are finite; a program needn't handle non-finite values.
Results may differ from a plain program's by a relative error of at most 0.013.
Values sent between devices are 32-bit elements; how exact they have to be, the bound alone decides.
No kernel may reach another device: no remote copies, remote signals or barrier semaphores. Data moves between devices by JAX's collectives and lax.ppermute only.
A program may use at most 64 MiB of HBM per device.

v0:
```python
import jax
import jax.numpy as jnp
from jax import lax
from jax.sharding import PartitionSpec as P

TILE_COLS = 256
ITERS = 3
EPS = 1e-06


def local_forward(tile_blocks, rows, cols, count, vector, tile_rows):
    width = tile_blocks.shape[-1]
    vec_b = vector.astype(jnp.bfloat16).reshape(-1, width)
    picked = jnp.take(vec_b, cols, axis=0)
    prod = jnp.einsum("kij,kj->ki", tile_blocks, picked, preferred_element_type=jnp.float32)
    live = (jnp.arange(tile_blocks.shape[0], dtype=jnp.int32) < count).astype(jnp.float32)
    prod = prod * live[:, None]
    return jax.ops.segment_sum(prod, rows, num_segments=tile_rows).reshape(-1)


def local_adjoint(tile_blocks, rows, cols, count, vector, tile_cols):
    width = tile_blocks.shape[-1]
    vec_b = vector.astype(jnp.bfloat16).reshape(-1, width)
    picked = jnp.take(vec_b, rows, axis=0)
    prod = jnp.einsum("kij,ki->kj", tile_blocks, picked, preferred_element_type=jnp.float32)
    live = (jnp.arange(tile_blocks.shape[0], dtype=jnp.int32) < count).astype(jnp.float32)
    prod = prod * live[:, None]
    return jax.ops.segment_sum(prod, cols, num_segments=tile_cols).reshape(-1)


def first_norm(data):
    return jnp.sqrt(lax.psum(jnp.sum(data * data), "row") + EPS)


def new_data_basis(partial_value, previous, alpha):
    summed = lax.psum(partial_value, "col")
    temp = summed - alpha * previous
    return (temp, None)


def new_model_basis(partial_value, previous, beta):
    summed = lax.psum(partial_value, "row")
    temp = summed - beta * previous
    alpha = jnp.sqrt(lax.psum(jnp.sum(temp * temp), "col") + EPS)
    return (temp / alpha, alpha)


def per_device(blocks, block_rows, block_cols, counts, data):
    tile_blocks = blocks[0, 0]
    rows = block_rows[0, 0]
    cols = block_cols[0, 0]
    count = counts[0, 0]
    width = tile_blocks.shape[-1]
    tile_rows = data.shape[0] // width
    tile_cols = TILE_COLS
    beta = first_norm(data)
    data_basis = data / beta
    zero_model = jnp.zeros((tile_cols * width,), jnp.float32)
    model_basis, alpha = new_model_basis(
        local_adjoint(tile_blocks, rows, cols, count, data_basis, tile_cols),
        zero_model,
        jnp.float32(0.0),
    )
    search = model_basis
    solution = zero_model
    phibar = beta
    rhobar = alpha
    for step in range(ITERS):
        partial_value = local_forward(tile_blocks, rows, cols, count, model_basis, tile_rows)
        temp, unused = new_data_basis(partial_value, data_basis, alpha)
        beta = first_norm(temp)
        data_basis = temp / beta
        partial_model = local_adjoint(tile_blocks, rows, cols, count, data_basis, tile_cols)
        model_basis, alpha = new_model_basis(partial_model, model_basis, beta)
        rho = jnp.sqrt(rhobar * rhobar + beta * beta)
        cosine = rhobar / rho
        sine = beta / rho
        theta = sine * alpha
        rhobar = -cosine * alpha
        phi = cosine * phibar
        phibar = sine * phibar
        solution = solution + phi / rho * search
        search = model_basis - theta / rho * search
    return (solution, search, data_basis)


def solution(mesh):
    in_specs = (
        P("row", "col", None, None, None),
        P("row", "col", None),
        P("row", "col", None),
        P("row", "col"),
        P("row"),
    )
    out_specs = (P("col"), P("col"), P("row"))
    return jax.shard_map(
        per_device, mesh=mesh, in_specs=in_specs, out_specs=out_specs, check_vma=False
    )
```

profile of v0, /device:TPU:0, one launch (start us, length us, event | category | flops | bytes accessed | tf_op | source)
XLA Modules:
  0.0 587.4 jit_solution(584488901513735829)
XLA Ops:
  7.2 0.7 compare_and_fusion.1
  7.9 0.7 compare_select_fusion.1
  8.6 1.5 multiply_reduce_fusion.7
  10.8 23.8 %psum.105 = f32[]{:T(128)} all-reduce(f32[]{:T(128)} %multiply_reduce_fusion.7), channel_id=1, replica_groups=mesh['row'=8,'col'=4] {'row'}, use_global_device_ids=true, to_apply=%region_1.0 | all-reduce | flops 1 | bytes 8 | tf_op jit(solution)/shard_map/psum | solution.py:32
  35.3 0.9 convert_bitcast_fusion.6
  36.2 0.9 gather_fusion
  37.1 0.1 select_bitcast_fusion.6
  37.2 5.7 fusion.12
  42.9 2.1 scatter_custom_fusion
  45.0 0.0 all-reduce.10.cloned.1.call-start
  45.1 67.8 %all-reduce.8.cloned.1.call-done = f32[32768]{0:T(1024)} async-done(((f32[32768]{0:T(1024)}), f32[32768]{0:T(1024)}) %all-reduce.8.cloned.1.call-update) | async-done | bytes 131088 | tf_op jit(solution)/shard_map/psum | solution.py:42
  112.9 1.5 multiply_reduce_fusion.6
  114.5 6.3 %psum.107 = f32[]{:T(128)} all-reduce(f32[]{:T(128)} %multiply_reduce_fusion.6), channel_id=1, replica_groups=mesh['row'=8,'col'=4] {'col'}, use_global_device_ids=true, to_apply=%region_5.7 | all-reduce | flops 1 | bytes 8 | tf_op jit(solution)/shard_map/psum | solution.py:44
  121.5 0.9 convert_bitcast_fusion.5
  122.4 0.9 gather_fusion.1
  123.2 0.1 select_bitcast_fusion.5
  123.4 7.8 %fusion.10 = f32[256,1,128]{2,1,0:T(1,128)S(1)} fusion(bf16[1,1,256,128,128]{4,3,2,1,0:T(8,128)(2,1)} %param.7, bf16[256,128,1]{1,0,2:T(8,128)(2,1)S(1)} %select_bitcast_fusion.5), kind=kOutput, calls=%fused_computation.24 | convolution fusion | flops 8388608 | bytes 8585216 | tf_op jit(solution)/shard_map/kij,kj->ki/dot_general | solution.py:15
  131.2 2.3 scatter_custom_fusion.1
  133.5 0.0 all-reduce.12.cloned.1.call-start
  133.5 31.3 %all-reduce.10.cloned.1.call-done = f32[32768]{0:T(1024)} async-done(((f32[32768]{0:T(1024)}), f32[32768]{0:T(1024)}) %all-reduce.10.cloned.1.call-update) | async-done | bytes 131088 | tf_op jit(solution)/shard_map/psum | solution.py:36
  164.8 1.6 multiply_reduce_fusion.5
  166.4 22.0 %psum.109 = f32[]{:T(128)} all-reduce(f32[]{:T(128)} %get-tuple-element.10), channel_id=1, replica_groups=mesh['row'=8,'col'=4] {'row'}, use_global_device_ids=true, to_apply=%region_9.11 | all-reduce | flops 1 | bytes 8 | tf_op jit(solution)/shard_map/psum | solution.py:32
  189.0 0.9 gather_fusion.2
  189.9 0.1 select_bitcast_fusion.4
  190.0 5.7 fusion.8
  195.7 2.1 scatter_custom_fusion.2
  197.8 0.0 all-reduce.14.cloned.1.call-start
  197.9 66.8 %all-reduce.12.cloned.1.call-done = f32[32768]{0:T(1024)} async-done(((f32[32768]{0:T(1024)}), f32[32768]{0:T(1024)}) %all-reduce.12.cloned.1.call-update) | async-done | bytes 131088 | tf_op jit(solution)/shard_map/psum | solution.py:42
  264.7 1.6 multiply_reduce_fusion.4
  266.3 6.4 %psum.111 = f32[]{:T(128)} all-reduce(f32[]{:T(128)} %multiply_reduce_fusion.4), channel_id=1, replica_groups=mesh['row'=8,'col'=4] {'col'}, use_global_device_ids=true, to_apply=%region_13.15 | all-reduce | flops 1 | bytes 8 | tf_op jit(solution)/shard_map/psum | solution.py:44
  273.4 0.9 convert_bitcast_fusion.3
  274.4 0.9 gather_fusion.3
  275.2 0.1 select_bitcast_fusion.3
  275.3 7.8 %fusion.6 = f32[256,1,128]{2,1,0:T(1,128)S(1)} fusion(bf16[1,1,256,128,128]{4,3,2,1,0:T(8,128)(2,1)} %param.7, bf16[256,128,1]{1,0,2:T(8,128)(2,1)S(1)} %select_bitcast_fusion.3), kind=kOutput, calls=%fused_computation.20 | convolution fusion | flops 8388608 | bytes 8585216 | tf_op jit(solution)/shard_map/kij,kj->ki/dot_general | solution.py:15
  283.1 2.3 scatter_custom_fusion.3
  285.4 0.0 all-reduce.16.cloned.1.call-start
  285.5 31.3 %all-reduce.14.cloned.1.call-done = f32[32768]{0:T(1024)} async-done(((f32[32768]{0:T(1024)}), f32[32768]{0:T(1024)}) %all-reduce.14.cloned.1.call-update) | async-done | bytes 131088 | tf_op jit(solution)/shard_map/psum | solution.py:36
  316.7 1.5 multiply_reduce_fusion.3
  318.3 22.0 %psum.113 = f32[]{:T(128)} all-reduce(f32[]{:T(128)} %get-tuple-element.6), channel_id=1, replica_groups=mesh['row'=8,'col'=4] {'row'}, use_global_device_ids=true, to_apply=%region_17.19 | all-reduce | flops 1 | bytes 8 | tf_op jit(solution)/shard_map/psum | solution.py:32
  341.0 0.9 gather_fusion.4
  341.8 0.1 select_bitcast_fusion.2
  341.9 5.7 fusion.4
  347.6 2.1 scatter_custom_fusion.4
  349.8 0.0 all-reduce.18.cloned.1.call-start
  349.8 66.8 %all-reduce.16.cloned.1.call-done = f32[32768]{0:T(1024)} async-done(((f32[32768]{0:T(1024)}), f32[32768]{0:T(1024)}) %all-reduce.16.cloned.1.call-update) | async-done | bytes 131088 | tf_op jit(solution)/shard_map/psum | solution.py:42
  416.6 1.5 multiply_reduce_fusion.2
  418.2 6.3 %psum.115 = f32[]{:T(128)} all-reduce(f32[]{:T(128)} %multiply_reduce_fusion.2), channel_id=1, replica_groups=mesh['row'=8,'col'=4] {'col'}, use_global_device_ids=true, to_apply=%region_21.23 | all-reduce | flops 1 | bytes 8 | tf_op jit(solution)/shard_map/psum | solution.py:44
  425.1 0.9 convert_bitcast_fusion.1
  426.1 0.9 gather_fusion.5
  426.9 0.1 select_bitcast_fusion.1
  427.1 7.8 %fusion.2 = f32[256,1,128]{2,1,0:T(1,128)S(1)} fusion(bf16[1,1,256,128,128]{4,3,2,1,0:T(8,128)(2,1)} %param.7, bf16[256,128,1]{1,0,2:T(8,128)(2,1)S(1)} %select_bitcast_fusion.1), kind=kOutput, calls=%fused_computation.16 | convolution fusion | flops 8388608 | bytes 8585216 | tf_op jit(solution)/shard_map/kij,kj->ki/dot_general | solution.py:15
  434.9 2.3 scatter_custom_fusion.5
  437.2 31.3 %all-reduce.18.cloned.1.call-done = f32[32768]{0:T(1024)} async-done(((f32[32768]{0:T(1024)}), f32[32768]{0:T(1024)}) %all-reduce.18.cloned.1.call-update) | async-done | bytes 131088 | tf_op jit(solution)/shard_map/psum | solution.py:36
  468.5 1.5 multiply_reduce_fusion.1
  470.0 22.2 %psum.117 = f32[]{:T(128)} all-reduce(f32[]{:T(128)} %multiply_reduce_fusion.1), channel_id=1, replica_groups=mesh['row'=8,'col'=4] {'row'}, use_global_device_ids=true, to_apply=%region_25.27 | all-reduce | flops 1 | bytes 8 | tf_op jit(solution)/shard_map/psum | solution.py:32
  492.9 1.6 convert_bitcast_fusion
  494.5 0.9 gather_fusion.6
  495.4 0.1 select_bitcast_fusion
  495.5 5.7 fusion
  501.1 2.1 scatter_custom_fusion.6
  503.9 66.3 %all-reduce.20.cloned.1.call-done = f32[32768]{0:T(1024)} async-done(((f32[32768]{0:T(1024)}), f32[32768]{0:T(1024)}) %all-reduce.20.cloned.1.call-update) | async-done | bytes 131088 | tf_op jit(solution)/shard_map/psum | solution.py:42
  570.2 1.6 multiply_reduce_fusion
  571.8 6.3 %psum.119 = f32[]{:T(128)} all-reduce(f32[]{:T(128)} %multiply_reduce_fusion), channel_id=1, replica_groups=mesh['row'=8,'col'=4] {'col'}, use_global_device_ids=true, to_apply=%region_29.31 | all-reduce | flops 1 | bytes 8 | tf_op jit(solution)/shard_map/psum | solution.py:44
  578.9 1.7 multiply_subtract_fusion
  (24 shorter events, 0.3 us)
Async XLA Ops:
  7.2 35.7 %copy-start.3 = (s32[1,1,256]{2,1,0:T(1,128)S(1)}, s32[1,1,256]{2,1,0:T(1,128)}, u32[]{:S(2)}) copy-start(s32[1,1,256]{2,1,0:T(1,128)} %param.9) | copy-start | bytes 3076
  7.2 105.8 %all-reduce.8.cloned.1.call-start = ((), (), s32[]{:S(2)}) async-start(), calls=%async_computation | async-start | bytes 262144 | tf_op jit(solution)/shard_map/psum | solution.py:42
  37.2 127.6 %copy-start.2 = (f32[32768]{0:T(1024)S(1)}, f32[32768]{0:T(1024)}, u32[]{:S(2)}) copy-start(f32[32768]{0:T(1024)} %param.11) | copy-start | bytes 393220
  45.0 119.8 %all-reduce.10.cloned.1.call-start = ((), (), s32[]{:S(2)}) async-start(), calls=%async_computation.1 | async-start | bytes 262144 | tf_op jit(solution)/shard_map/psum | solution.py:36
  123.4 141.4 %copy-start = (f32[32768]{0:T(1024)S(1)}, f32[32768]{0:T(1024)}, u32[]{:S(2)}) copy-start(f32[32768]{0:T(1024)} %all-reduce.8.cloned.1.call-done) | copy-start | bytes 393220
  133.5 131.2 %all-reduce.12.cloned.1.call-start = ((), (), s32[]{:S(2)}) async-start(), calls=%async_computation.2 | async-start | bytes 262144 | tf_op jit(solution)/shard_map/psum | solution.py:42
  197.8 118.9 %all-reduce.14.cloned.1.call-start = ((), (), s32[]{:S(2)}) async-start(), calls=%async_computation.3 | async-start | bytes 262144 | tf_op jit(solution)/shard_map/psum | solution.py:36
  285.4 131.2 %all-reduce.16.cloned.1.call-start = ((), (), s32[]{:S(2)}) async-start(), calls=%async_computation.4 | async-start | bytes 262144 | tf_op jit(solution)/shard_map/psum | solution.py:42
  349.8 118.7 %all-reduce.18.cloned.1.call-start = ((), (), s32[]{:S(2)}) async-start(), calls=%async_computation.5 | async-start | bytes 262144 | tf_op jit(solution)/shard_map/psum | solution.py:36
  427.0 143.2 %copy-start.1 = (f32[32768]{0:T(1024)S(1)}, f32[32768]{0:T(1024)}, u32[]{:S(2)}) copy-start(f32[32768]{0:T(1024)} %all-reduce.16.cloned.1.call-done) | copy-start | bytes 393220
  437.2 133.0 %all-reduce.20.cloned.1.call-start = ((), (), s32[]{:S(2)}) async-start(), calls=%async_computation.6 | async-start | bytes 262144 | tf_op jit(solution)/shard_map/psum | solution.py:42
Sparse Core Ops, SparseCore 0:
  45.1 67.7 all-reduce.7
  133.6 31.1 all-reduce.9
  197.9 66.7 all-reduce.11
  285.5 31.1 all-reduce.13
  349.9 66.7 all-reduce.15
  437.3 31.1 all-reduce.17
  503.4 66.7 all-reduce.19
where the time goes:
time: 588 us; the launch traced here: 587 us
  waiting for transfers between devices  362 us (62%)
  blocking collectives  115 us (20%)
  matrix products  46 us (8%)
  other arithmetic  37 us (6%)
  between operations  21.2 us (4%)
  local copies, waits for them, and re-layouts  6.01 us (1%)
    psum x4, waiting for transfers between devices, new_model_basis(): summed = lax.psum(partial_value, 'row')  268 us
    psum x3, waiting for transfers between devices, new_data_basis(): summed = lax.psum(partial_value, 'col')  93.8 us
    psum x4, blocking collectives, first_norm(): return jnp.sqrt(lax.psum(jnp.sum(data * data), 'row') + EPS)  89.9 us
    psum x4, blocking collectives, new_model_basis(): alpha = jnp.sqrt(lax.psum(jnp.sum(temp * temp), 'col') + EPS)  25.3 us
    dot_general x3, matrix products, local_forward(): jnp.einsum('kij,kj->ki', tile_blocks, picked, preferred_element_type=jnp....  23.4 us
    dot_general x4, matrix products, local_adjoint(): jnp.einsum('kij,ki->kj', tile_blocks, picked, preferred_element_type=jnp....  22.6 us
  transfers between devices with their start and end apart: 7, of which 7 were waited for; matrix products, arithmetic and copies ran while one was open for 0% of the time, Pallas kernels for 0%

commit v1 on v0

--- a/solution.py
+++ b/solution.py
@@ -33,7 +33,7 @@
 
 
 def new_data_basis(partial_value, previous, alpha):
-    summed = lax.psum(partial_value, "col")
+    summed = jnp.sum(lax.all_gather(partial_value, "col"), axis=0)
     temp = summed - alpha * previous
     return (temp, None)
 

time: 588 us -> 508 us (0.86)
  waiting for transfers between devices: 362 us -> 269 us
  blocking collectives: 115 us -> 132 us
    psum x3 -> x0, waiting for transfers between devices: 93.8 us -> none  [new_data_basis(): summed = lax.psum(partial_value, 'col')]
    all_gather x0 -> x3, blocking collectives: none -> 22.2 us  [new_data_basis(): summed = jnp.sum(lax.all_gather(partial_value, 'col'), axis=0)]
  transfers between devices with their start and end apart: 7 -> 4, of which waited for: 7 -> 4; matrix products, arithmetic and copies ran while one was open for 0% -> 0% of each run, Pallas kernels for 0% -> 0%
where the time goes in v1:
time: 508 us; the launch traced here: 507 us
  waiting for transfers between devices  269 us (53%)
  blocking collectives  132 us (26%)
  matrix products  46 us (9%)
  other arithmetic  33.1 us (7%)
  between operations  20.8 us (4%)
  local copies, waits for them, and re-layouts  6.01 us (1%)
    psum x4, waiting for transfers between devices, new_model_basis(): summed = lax.psum(partial_value, 'row')  269 us
    psum x4, blocking collectives, first_norm(): return jnp.sqrt(lax.psum(jnp.sum(data * data), 'row') + EPS)  84.4 us
    psum x4, blocking collectives, new_model_basis(): alpha = jnp.sqrt(lax.psum(jnp.sum(temp * temp), 'col') + EPS)  25.3 us
    dot_general x3, matrix products, local_forward(): jnp.einsum('kij,kj->ki', tile_blocks, picked, preferred_element_type=jnp....  23.4 us
    dot_general x4, matrix products, local_adjoint(): jnp.einsum('kij,ki->kj', tile_blocks, picked, preferred_element_type=jnp....  22.6 us
    all_gather x3, blocking collectives, new_data_basis(): summed = jnp.sum(lax.all_gather(partial_value, 'col'), axis=0)  22.2 us
  transfers between devices with their start and end apart: 4, of which 4 were waited for; matrix products, arithmetic and copies ran while one was open for 0% of the time, Pallas kernels for 0%

profile of v1, /device:TPU:0, one launch (start us, length us, event | category | flops | bytes accessed | tf_op | source)
XLA Modules:
  0.0 507.1 jit_solution(15202003990289084342)
XLA Ops:
  7.2 1.5 multiply_reduce_fusion.7
  8.8 0.7 compare_select_fusion.1
  9.4 0.7 compare_and_fusion.1
  10.1 23.7 %psum.84 = f32[]{:T(128)} all-reduce(f32[]{:T(128)} %multiply_reduce_fusion.7), channel_id=1, replica_groups=mesh['row'=8,'col'=4] {'row'}, use_global_device_ids=true, to_apply=%region_1.0 | all-reduce | flops 1 | bytes 8 | tf_op jit(solution)/shard_map/psum | solution.py:32
  34.6 0.9 convert_bitcast_fusion.6
  36.2 0.9 gather_fusion
  37.0 0.1 select_bitcast_fusion.6
  37.1 5.7 %fusion.12 = f32[256,1,128]{2,1,0:T(1,128)S(1)} fusion(bf16[1,1,256,128,128]{4,3,2,1,0:T(8,128)(2,1)} %param.7, bf16[256,128,1]{1,0,2:T(8,128)(2,1)S(1)} %select_bitcast_fusion.6), kind=kOutput, calls=%fused_computation.26 | convolution fusion | flops 8388608 | bytes 8585216 | tf_op jit(solution)/shard_map/kij,ki->kj/dot_general | solution.py:25
  42.8 2.1 scatter_custom_fusion
  45.1 67.8 %all-reduce.5.cloned.1.call-done = f32[32768]{0:T(1024)} async-done(((f32[32768]{0:T(1024)}), f32[32768]{0:T(1024)}) %all-reduce.5.cloned.1.call-update) | async-done | bytes 131088 | tf_op jit(solution)/shard_map/psum | solution.py:42
  112.9 1.5 multiply_reduce_fusion.6
  114.5 6.3 %psum.86 = f32[]{:T(128)} all-reduce(f32[]{:T(128)} %multiply_reduce_fusion.6), channel_id=1, replica_groups=mesh['row'=8,'col'=4] {'col'}, use_global_device_ids=true, to_apply=%region_5.7 | all-reduce | flops 1 | bytes 8 | tf_op jit(solution)/shard_map/psum | solution.py:44
  121.4 0.9 convert_bitcast_fusion.5
  122.4 0.9 gather_fusion.1
  123.2 0.1 select_bitcast_fusion.5
  123.3 7.8 %fusion.10 = f32[256,1,128]{2,1,0:T(1,128)S(1)} fusion(bf16[1,1,256,128,128]{4,3,2,1,0:T(8,128)(2,1)} %param.7, bf16[256,128,1]{1,0,2:T(8,128)(2,1)S(1)} %select_bitcast_fusion.5), kind=kOutput, calls=%fused_computation.24 | convolution fusion | flops 8388608 | bytes 8585216 | tf_op jit(solution)/shard_map/kij,kj->ki/dot_general | solution.py:15
  131.1 1.7 scatter_custom_fusion.1
  132.9 7.4 %all-gather = f32[4,1,32768]{2,1,0:T(1,128)S(1)} all-gather(f32[1,1,32768]{2,1,0:T(1,128)S(1)} %bitcast.75), channel_id=1, replica_groups=mesh['row'=8,'col'=4] {'col'}, dimensions={0}, use_global_device_ids=true | all-gather | bytes 655360 | tf_op jit(solution)/shard_map/all_gather | solution.py:36
  140.3 0.5 reduce_sum.101
  140.8 0.6 multiply_reduce_fusion.5
  141.4 20.2 %psum.87 = f32[]{:T(128)} all-reduce(f32[]{:T(128)} %get-tuple-element.10), channel_id=1, replica_groups=mesh['row'=8,'col'=4] {'row'}, use_global_device_ids=true, to_apply=%region_9.11 | all-reduce | flops 1 | bytes 8 | tf_op jit(solution)/shard_map/psum | solution.py:32
  162.3 0.9 gather_fusion.2
  163.2 0.1 select_bitcast_fusion.4
  163.3 5.7 %fusion.8 = f32[256,1,128]{2,1,0:T(1,128)S(1)} fusion(bf16[1,1,256,128,128]{4,3,2,1,0:T(8,128)(2,1)} %param.7, bf16[256,128,1]{1,0,2:T(8,128)(2,1)S(1)} %select_bitcast_fusion.4), kind=kOutput, calls=%fused_computation.22 | convolution fusion | flops 8388608 | bytes 8585216 | tf_op jit(solution)/shard_map/kij,ki->kj/dot_general | solution.py:25
  168.9 2.1 scatter_custom_fusion.2
  171.1 0.0 all-reduce.9.cloned.1.call-start
  171.1 67.2 %all-reduce.7.cloned.1.call-done = f32[32768]{0:T(1024)} async-done(((f32[32768]{0:T(1024)}), f32[32768]{0:T(1024)}) %all-reduce.7.cloned.1.call-update) | async-done | bytes 131088 | tf_op jit(solution)/shard_map/psum | solution.py:42
  238.4 1.6 multiply_reduce_fusion.4
  239.9 6.4 %psum.89 = f32[]{:T(128)} all-reduce(f32[]{:T(128)} %multiply_reduce_fusion.4), channel_id=1, replica_groups=mesh['row'=8,'col'=4] {'col'}, use_global_device_ids=true, to_apply=%region_13.15 | all-reduce | flops 1 | bytes 8 | tf_op jit(solution)/shard_map/psum | solution.py:44
  247.1 0.9 convert_bitcast_fusion.3
  248.0 0.9 gather_fusion.3
  248.9 0.1 select_bitcast_fusion.3
  249.0 7.8 %fusion.6 = f32[256,1,128]{2,1,0:T(1,128)S(1)} fusion(bf16[1,1,256,128,128]{4,3,2,1,0:T(8,128)(2,1)} %param.7, bf16[256,128,1]{1,0,2:T(8,128)(2,1)S(1)} %select_bitcast_fusion.3), kind=kOutput, calls=%fused_computation.20 | convolution fusion | flops 8388608 | bytes 8585216 | tf_op jit(solution)/shard_map/kij,kj->ki/dot_general | solution.py:15
  256.8 1.7 scatter_custom_fusion.3
  258.5 7.4 %all-gather.1 = f32[4,1,32768]{2,1,0:T(1,128)S(1)} all-gather(f32[1,1,32768]{2,1,0:T(1,128)S(1)} %bitcast.76), channel_id=1, replica_groups=mesh['row'=8,'col'=4] {'col'}, dimensions={0}, use_global_device_ids=true | all-gather | bytes 655360 | tf_op jit(solution)/shard_map/all_gather | solution.py:36
  265.9 0.5 reduce_sum.104
  266.4 0.6 multiply_reduce_fusion.3
  267.0 20.2 %psum.90 = f32[]{:T(128)} all-reduce(f32[]{:T(128)} %get-tuple-element.6), channel_id=1, replica_groups=mesh['row'=8,'col'=4] {'row'}, use_global_device_ids=true, to_apply=%region_17.19 | all-reduce | flops 1 | bytes 8 | tf_op jit(solution)/shard_map/psum | solution.py:32
  287.9 0.9 gather_fusion.4
  288.8 0.1 select_bitcast_fusion.2
  288.9 5.7 %fusion.4 = f32[256,1,128]{2,1,0:T(1,128)S(1)} fusion(bf16[1,1,256,128,128]{4,3,2,1,0:T(8,128)(2,1)} %param.7, bf16[256,128,1]{1,0,2:T(8,128)(2,1)S(1)} %select_bitcast_fusion.2), kind=kOutput, calls=%fused_computation.18 | convolution fusion | flops 8388608 | bytes 8585216 | tf_op jit(solution)/shard_map/kij,ki->kj/dot_general | solution.py:25
  294.5 2.1 scatter_custom_fusion.4
  296.7 0.0 all-reduce.11.cloned.1.call-start
  296.7 67.2 %all-reduce.9.cloned.1.call-done = f32[32768]{0:T(1024)} async-done(((f32[32768]{0:T(1024)}), f32[32768]{0:T(1024)}) %all-reduce.9.cloned.1.call-update) | async-done | bytes 131088 | tf_op jit(solution)/shard_map/psum | solution.py:42
  363.9 1.5 multiply_reduce_fusion.2
  365.5 6.3 %psum.92 = f32[]{:T(128)} all-reduce(f32[]{:T(128)} %multiply_reduce_fusion.2), channel_id=1, replica_groups=mesh['row'=8,'col'=4] {'col'}, use_global_device_ids=true, to_apply=%region_21.23 | all-reduce | flops 1 | bytes 8 | tf_op jit(solution)/shard_map/psum | solution.py:44
  372.5 0.9 convert_bitcast_fusion.1
  373.4 0.9 gather_fusion.5
  374.2 0.1 select_bitcast_fusion.1
  374.4 7.8 %fusion.2 = f32[256,1,128]{2,1,0:T(1,128)S(1)} fusion(bf16[1,1,256,128,128]{4,3,2,1,0:T(8,128)(2,1)} %param.7, bf16[256,128,1]{1,0,2:T(8,128)(2,1)S(1)} %select_bitcast_fusion.1), kind=kOutput, calls=%fused_computation.16 | convolution fusion | flops 8388608 | bytes 8585216 | tf_op jit(solution)/shard_map/kij,kj->ki/dot_general | solution.py:15
  382.2 1.7 scatter_custom_fusion.5
  383.9 7.4 %all-gather.2 = f32[4,1,32768]{2,1,0:T(1,128)S(1)} all-gather(f32[1,1,32768]{2,1,0:T(1,128)S(1)} %bitcast.77), channel_id=1, replica_groups=mesh['row'=8,'col'=4] {'col'}, dimensions={0}, use_global_device_ids=true | all-gather | bytes 655360 | tf_op jit(solution)/shard_map/all_gather | solution.py:36
  391.3 0.5 reduce_sum.107
  391.8 0.6 multiply_reduce_fusion.1
  392.4 20.4 %psum.93 = f32[]{:T(128)} all-reduce(f32[]{:T(128)} %multiply_reduce_fusion.1), channel_id=1, replica_groups=mesh['row'=8,'col'=4] {'row'}, use_global_device_ids=true, to_apply=%region_25.27 | all-reduce | flops 1 | bytes 8 | tf_op jit(solution)/shard_map/psum | solution.py:32
  413.5 0.7 convert_bitcast_fusion
  414.2 0.9 gather_fusion.6
  415.1 0.1 select_bitcast_fusion
  415.2 5.7 %fusion = f32[256,1,128]{2,1,0:T(1,128)S(1)} fusion(bf16[1,1,256,128,128]{4,3,2,1,0:T(8,128)(2,1)} %param.7, bf16[256,128,1]{1,0,2:T(8,128)(2,1)S(1)} %select_bitcast_fusion), kind=kOutput, calls=%fused_computation.14 | convolution fusion | flops 8388608 | bytes 8585216 | tf_op jit(solution)/shard_map/kij,ki->kj/dot_general | solution.py:25
  420.8 2.1 scatter_custom_fusion.6
  423.6 66.7 %all-reduce.11.cloned.1.call-done = f32[32768]{0:T(1024)} async-done(((f32[32768]{0:T(1024)}), f32[32768]{0:T(1024)}) %all-reduce.11.cloned.1.call-update) | async-done | bytes 131088 | tf_op jit(solution)/shard_map/psum | solution.py:42
  490.3 1.6 multiply_reduce_fusion
  491.9 6.3 %psum.95 = f32[]{:T(128)} all-reduce(f32[]{:T(128)} %multiply_reduce_fusion), channel_id=1, replica_groups=mesh['row'=8,'col'=4] {'col'}, use_global_device_ids=true, to_apply=%region_29.31 | all-reduce | flops 1 | bytes 8 | tf_op jit(solution)/shard_map/psum | solution.py:44
  498.9 1.7 multiply_subtract_fusion
  (21 shorter events, 0.2 us)
Async XLA Ops:
  7.2 35.7 %copy-start.3 = (s32[1,1,256]{2,1,0:T(1,128)S(1)}, s32[1,1,256]{2,1,0:T(1,128)}, u32[]{:S(2)}) copy-start(s32[1,1,256]{2,1,0:T(1,128)} %param.9) | copy-start | bytes 3076
  7.2 105.7 %all-reduce.5.cloned.1.call-start = ((), (), s32[]{:S(2)}) async-start(), calls=%async_computation | async-start | bytes 262144 | tf_op jit(solution)/shard_map/psum | solution.py:42
  37.1 103.6 %copy-start.2 = (f32[32768]{0:T(1024)S(1)}, f32[32768]{0:T(1024)}, u32[]{:S(2)}) copy-start(f32[32768]{0:T(1024)} %param.11) | copy-start | bytes 393220
  45.0 193.4 %all-reduce.7.cloned.1.call-start = ((), (), s32[]{:S(2)}) async-start(), calls=%async_computation.1 | async-start | bytes 262144 | tf_op jit(solution)/shard_map/psum | solution.py:42
  123.3 115.1 %copy-start = (f32[32768]{0:T(1024)S(1)}, f32[32768]{0:T(1024)}, u32[]{:S(2)}) copy-start(f32[32768]{0:T(1024)} %all-reduce.5.cloned.1.call-done) | copy-start | bytes 393220
  171.1 192.9 %all-reduce.9.cloned.1.call-start = ((), (), s32[]{:S(2)}) async-start(), calls=%async_computation.2 | async-start | bytes 262144 | tf_op jit(solution)/shard_map/psum | solution.py:42
  296.7 193.6 %all-reduce.11.cloned.1.call-start = ((), (), s32[]{:S(2)}) async-start(), calls=%async_computation.3 | async-start | bytes 262144 | tf_op jit(solution)/shard_map/psum | solution.py:42
  374.4 115.9 %copy-start.1 = (f32[32768]{0:T(1024)S(1)}, f32[32768]{0:T(1024)}, u32[]{:S(2)}) copy-start(f32[32768]{0:T(1024)} %all-reduce.9.cloned.1.call-done) | copy-start | bytes 393220
Sparse Core Ops, SparseCore 0:
  45.1 67.7 all-reduce.4
  171.2 67.1 all-reduce.6
  296.8 67.0 all-reduce.8
  423.1 67.1 all-reduce.10
